TPU v7x, 32 devices: a whole 2x2x4 slice. The times are simulated.
32 devices in a mesh: runs: 2 (over y), gz: 4 (over x, core), gx: 4 (over z).
Axes of the slice: x: 2, y: 2, z: 4, core: 2. Of those that a mesh axis runs over, the one named last changes fastest.
Arguments:
- magnetic: float32 [3, 64, 64, 1024], P(None, 'gx', 'gz', 'runs'), parts along dimension 3, may hold values from -12 to 12
- friction: float32 [64], P('gz'), may hold values from 0.3 to 3
Outputs:
- relaxed: float32 [3, 64, 64, 1024], P(None, 'gx', 'gz', 'runs'), parts along dimension 3
- potential: float32 [3, 64, 64, 1024], P(None, 'gx', 'gz', 'runs'), parts along dimension 3
There are 2 independent parts, one for each index of `runs`. A program takes and returns all parts, laid end to end along the dimension named above; an argument that names none is the same for every part. Nothing has to cross between parts.
All inputs are finite; a program needn't handle non-finite values.
Results may differ from a plain program's by a relative error of at most 0.00017.
Values sent between devices are 32-bit elements; how exact they have to be, the bound alone decides.
A program may use at most 64 MiB of HBM per device.

v0:
```python
import functools

import jax
import jax.numpy as jnp
from jax import lax
from jax.experimental import pallas as pl
from jax.experimental.pallas import tpu as pltpu
from jax.sharding import PartitionSpec as P

DESCENTS = 2
RELAX = 2
ROUNDS = 1 + (DESCENTS - 1) + RELAX
LANES = 128

step_scale = 0.5
time_step = 0.2

DIRS = ((-1, 0), (1, 0), (0, -1), (0, 1), (-1, -1), (-1, 1), (1, -1), (1, 1))
OPP = (1, 0, 3, 2, 7, 6, 5, 4)


def cross(l, r):
    return [l[1] * r[2] - l[2] * r[1], l[2] * r[0] - l[0] * r[2], l[0] * r[1] - l[1] * r[0]]


def dot(l, r):
    return l[0] * r[0] + l[1] * r[1] + l[2] * r[2]


def kernel(
    gxn, gzn, cx, cz, nb, mag, fric, out_r, out_p,
    fld, pot, fb, eb, xr, zs, zr, cs, cr, ps, pr, ts, tr, above,
    ssem, rsem, psend, precv, tsend, trecv, insem, osem,
):
    gx = lax.axis_index("gx")
    gz = lax.axis_index("gz")
    n = gxn * gzn
    me = gz * gxn + gx
    core = pl.ds(8, cz)
    rim = cz + 8
    f32 = jnp.float32

    def lanes(b):
        return pl.ds(b * LANES, LANES)

    def in_copy(b):
        return pltpu.make_async_copy(
            mag.at[:, :, :, lanes(b)], fld.at[:, pl.ds(2, cx), b, core, :], insem.at[b]
        )

    for b in range(nb):
        in_copy(b).start()

    barrier = pltpu.get_barrier_semaphore()

    def peer(j):
        other = (me + j) % n
        return {"gz": other // gxn, "gx": other % gxn}

    def greet(j, _):
        pl.semaphore_signal(barrier, inc=1, device_id=peer(j), device_id_type=pl.DeviceIdType.MESH)
        return 0

    lax.fori_loop(1, n, greet, 0)

    for ref in (fld, pot):
        for c in range(3):
            for i in (0, 1, cx + 2, cx + 3):
                ref[c, i] = jnp.zeros(ref.shape[2:], f32)

        def clear(i, _):
            for c in range(3):
                for b in range(nb):
                    ref[c, i, b, 0:8, :] = jnp.zeros((8, LANES), f32)
                    ref[c, i, b, cz + 8 : cz + 16, :] = jnp.zeros((8, LANES), f32)
            return 0

        lax.fori_loop(2, cx + 2, clear, 0)

    pl.semaphore_wait(barrier, n - 1)
    for b in range(nb):
        in_copy(b).wait()

    def exists(d):
        dx, dz = DIRS[d]
        tests = []
        if dx:
            tests.append(gx > 0 if dx < 0 else gx < gxn - 1)
        if dz:
            tests.append(gz > 0 if dz < 0 else gz < gzn - 1)
        return functools.reduce(jnp.logical_and, tests)

    def link(r, d, src):
        dx, dz = DIRS[d]
        o = OPP[d]
        if d < 2:
            start = 2 if d == 0 else cx
            s, t = src.at[:, pl.ds(start, 2), :, core, :], xr.at[r, o]
        elif d < 4:
            s, t = zs.at[r, d - 2], zr.at[r, o - 2]
        else:
            s, t = cs.at[r, d - 4], cr.at[r, o - 4]
        return pltpu.make_async_remote_copy(
            src_ref=s, dst_ref=t, send_sem=ssem.at[r, d], recv_sem=rsem.at[r, o],
            device_id={"gz": gz + dz, "gx": gx + dx}, device_id_type=pl.DeviceIdType.MESH,
        )

    def arrival(r, d, src):
        dx, dz = DIRS[d]
        if d < 2:
            s, t = src.at[:, pl.ds(2, 2), :, core, :], xr.at[r, d]
        elif d < 4:
            s, t = zs.at[r, d - 2], zr.at[r, d - 2]
        else:
            s, t = cs.at[r, d - 4], cr.at[r, d - 4]
        return pltpu.make_async_remote_copy(
            src_ref=s, dst_ref=t, send_sem=ssem.at[r, d], recv_sem=rsem.at[r, d],
            device_id={"gz": gz + dz, "gx": gx + dx}, device_id_type=pl.DeviceIdType.MESH,
        )

    def send_halo(r, src):
        for d in (0, 1):
            @pl.when(exists(d))
            def _(d=d):
                link(r, d, src).start()

        def pack(i, _):
            for c in range(3):
                for b in range(nb):
                    zs[r, 0, c, i, 2 * b : 2 * b + 2, :] = src[c, i + 2, b, 8:10, :]
                    zs[r, 1, c, i, 2 * b : 2 * b + 2, :] = src[c, i + 2, b, cz + 6 : cz + 8, :]
            return 0

        lax.fori_loop(0, cx, pack, 0)
        for d in range(4, 8):
            dx, dz = DIRS[d]
            i = 2 if dx < 0 else cx + 1
            k = 8 if dz < 0 else cz + 7
            for c in range(3):
                for b in range(nb):
                    cs[r, d - 4, c, b : b + 1, :] = src[c, i, b, k : k + 1, :]
        for d in range(2, 8):
            @pl.when(exists(d))
            def _(d=d):
                link(r, d, src).start()

    def take_halo(r, src, dst, mu):
        def put(old, new):
            return new if mu is None else old + mu * new

        for d in (2, 3, 4, 5, 6, 7, 0, 1):
            dx, dz = DIRS[d]

            @pl.when(exists(d))
            def _(d=d, dx=dx, dz=dz):
                arrival(r, d, src).wait_recv()
                if d < 2:
                    base = 0 if d == 0 else cx + 2
                    for c in range(3):
                        for p in range(2):
                            for b in range(nb):
                                dst[c, base + p, b, core, :] = put(dst[c, base + p, b, core, :], xr[r, d, c, p, b])
                elif d < 4:
                    row = 6 if d == 2 else cz + 8

                    def unpack(i, _):
                        for c in range(3):
                            for b in range(nb):
                                dst[c, i + 2, b, row : row + 2, :] = put(
                                    dst[c, i + 2, b, row : row + 2, :], zr[r, d - 2, c, i, 2 * b : 2 * b + 2, :]
                                )
                        return 0

                    lax.fori_loop(0, cx, unpack, 0)
                else:
                    i = 1 if dx < 0 else cx + 2
                    k = 7 if dz < 0 else cz + 8
                    for c in range(3):
                        for b in range(nb):
                            dst[c, i, b, k : k + 1, :] = put(dst[c, i, b, k : k + 1, :], cr[r, d - 4, c, b : b + 1, :])
                link(r, d, src).wait_send()

    def differ(ref, comps, i, r0, rows, lane):
        first, last = lane == 0, lane == LANES - 1
        mid = {c: [ref[c, i, b, pl.ds(r0, rows), :] for b in range(nb)] for c in comps}

        def dy(c, b):
            here = mid[c][b]
            nxt, prv = mid[c][(b + 1) % nb], mid[c][(b - 1) % nb]
            up = pltpu.roll(jnp.where(first, nxt, here), LANES - 1, 1)
            down = pltpu.roll(jnp.where(last, prv, here), 1, 1)
            return up - down

        def dx(c, b):
            return ref[c, i + 1, b, pl.ds(r0, rows), :] - ref[c, i - 1, b, pl.ds(r0, rows), :]

        def dz(c, b):
            return ref[c, i, b, pl.ds(r0 + 1, rows), :] - ref[c, i, b, pl.ds(r0 - 1, rows), :]

        return mid, dx, dy, dz

    def folded(v):
        total = v[0:8]
        for k in range(8, v.shape[0], 8):
            total = total + v[k : k + 8]
        return total

    lane_rim = lax.broadcasted_iota(jnp.int32, (rim, LANES), 1)
    row_rim = lax.broadcasted_iota(jnp.int32, (rim, LANES), 0)
    lane_core = lax.broadcasted_iota(jnp.int32, (cz, LANES), 1)
    row_core = lax.broadcasted_iota(jnp.int32, (cz, LANES), 0)
    rows_in = (row_rim >= 1) & (row_rim <= cz)

    def omega_plane(i, acc):
        mid, dx, dy, dz = differ(fld, (0, 1, 2), i, 7, rim, lane_rim)
        rows = pl.ds(7, rim)
        inner = rows_in & ((i >= 2) & (i < cx + 2))
        for b in range(nb):
            B = [mid[c][b] for c in range(3)]
            J = [
                0.5 * (dy(2, b) - dz(1, b)),
                0.5 * (dz(0, b) - dx(2, b)),
                0.5 * (dx(1, b) - dy(0, b)),
            ]
            D = 0.5 * (dx(0, b) + dy(1, b) + dz(2, b))
            inv = 1.0 / jnp.maximum(dot(B, B), 1.0)
            L = cross(J, B)
            om = [(L[c] - D * B[c]) * inv for c in range(3)]
            E = cross(om, B)
            for c in range(3):
                eb[c, i, b, rows, :] = E[c]
            eb[3, i, b, rows, :] = dot(om, B)
            oj = cross(om, J)
            oo = dot(om, om)
            for c in range(3):
                fb[c, i, b, rows, :] = om[c] * D - oj[c] + oo * B[c]
            acc = acc + folded(jnp.where(inner, dot(L, L) * inv + D * D, 0.0))
        return acc

    def force_plane(i, acc):
        mid, dx, dy, dz = differ(eb, (0, 1, 2, 3), i, 8, cz, lane_core)
        for b in range(nb):
            curl = [
                dy(2, b) - dz(1, b) - dx(3, b),
                dz(0, b) - dx(2, b) - dy(3, b),
                dx(1, b) - dy(0, b) - dz(3, b),
            ]
            F = [fb[c, i, b, core, :] + 0.5 * curl[c] for c in range(3)]
            for c in range(3):
                fb[c, i, b, core, :] = F[c]
            acc = acc + folded(dot(F, F))
        return acc

    def psum_copy(s, slot, j):
        return pltpu.make_async_remote_copy(
            src_ref=ps.at[s], dst_ref=pr.at[s, slot], send_sem=psend.at[s, j], recv_sem=precv.at[s, slot],
            device_id=peer(j), device_id_type=pl.DeviceIdType.MESH,
        )

    def send_sums(s, lsum, gsum):
        ps[s, 0:1, :] = jnp.sum(lsum, axis=0, keepdims=True)
        ps[s, 1:2, :] = jnp.sum(gsum, axis=0, keepdims=True)

        def go(j, _):
            psum_copy(s, me, j).start()
            return 0

        lax.fori_loop(1, n, go, 0)

    def take_sums(s):
        pr[s, me] = ps[s]

        def arrive(j, _):
            psum_copy(s, (me + j) % n, j).wait_recv()
            return 0

        lax.fori_loop(1, n, arrive, 0)
        total = lax.fori_loop(0, n, lambda k, t: t + pr[s, k], jnp.zeros((2, LANES), f32))

        def left(j, _):
            psum_copy(s, me, j).wait_send()
            return 0

        lax.fori_loop(1, n, left, 0)
        sums = jnp.sum(total, axis=1, keepdims=True) / (n * cx * cz * nb * LANES)
        return step_scale * sums[0:1] / (sums[1:2] + 1e-6)

    send_halo(0, fld)
    take_halo(0, fld, fld, None)
    zero = jnp.zeros((8, LANES), f32)
    for s in range(DESCENTS):
        lsum = lax.fori_loop(1, cx + 3, omega_plane, zero)
        gsum = lax.fori_loop(2, cx + 2, force_plane, zero)
        send_sums(s, lsum, gsum)
        if s < DESCENTS - 1:
            send_halo(s + 1, fb)
        mu = take_sums(s)

        def update(i, _):
            for c in range(3):
                for b in range(nb):
                    fld[c, i, b, core, :] = fld[c, i, b, core, :] + mu * fb[c, i, b, core, :]
            return 0

        lax.fori_loop(2, cx + 2, update, 0)
        if s < DESCENTS - 1:
            take_halo(s + 1, fb, fld, mu)

    def out_copy(src, out, b, k):
        return pltpu.make_async_copy(
            src.at[:, pl.ds(2, cx), b, core, :], out.at[:, :, :, lanes(b)], osem.at[k, b]
        )

    for b in range(nb):
        out_copy(fld, out_r, b, 0).start()

    def suffix_plane(i, _):
        for c, other, sign in ((0, 1, -1.0), (1, 0, 1.0)):
            for b in range(nb):
                v = sign * fld[other, i, b, core, :]
                step = 1
                while step < cz:
                    v = v + jnp.where(row_core < cz - step, pltpu.roll(v, cz - step, 0), 0.0)
                    step *= 2
                pot[c, i, b, core, :] = v
                ts[c, i - 2, b : b + 1, :] = v[0:1]
        for b in range(nb):
            pot[2, i, b, core, :] = jnp.zeros((cz, LANES), f32)
        return 0

    lax.fori_loop(2, cx + 2, suffix_plane, 0)

    def column_copy(k, dz):
        return pltpu.make_async_remote_copy(
            src_ref=ts, dst_ref=tr.at[k], send_sem=tsend.at[k], recv_sem=trecv.at[k],
            device_id={"gz": gz + dz, "gx": gx}, device_id_type=pl.DeviceIdType.MESH,
        )

    for k in range(1, gzn):
        @pl.when(gz - k >= 0)
        def _(k=k):
            column_copy(k - 1, -k).start()

    above[...] = jnp.zeros(above.shape, f32)
    for k in range(1, gzn):
        @pl.when(gz + k < gzn)
        def _(k=k):
            column_copy(k - 1, k).wait_recv()
            above[...] = above[...] + tr[k - 1]

    def lift(i, _):
        for c in range(2):
            for b in range(nb):
                pot[c, i, b, core, :] = pot[c, i, b, core, :] + above[c, i - 2, b : b + 1, :]
        return 0

    lax.fori_loop(2, cx + 2, lift, 0)
    for k in range(1, gzn):
        @pl.when(gz - k >= 0)
        def _(k=k):
            column_copy(k - 1, -k).wait_send()

    drag = jnp.zeros((cz, LANES), f32)
    for k in range(cz):
        drag = jnp.where(row_core == k, fric[k], drag)
    z_at = gz * cz + row_rim - 1
    z_in = (z_at >= 0) & (z_at < gzn * cz)

    def induced_plane(i, _):
        mid, dx, dy, dz = differ(pot, (0, 1, 2), i, 7, rim, lane_rim)
        x_at = gx * cx + i - 2
        factor = jnp.where(z_in & ((x_at >= 0) & (x_at < gxn * cx)), 0.5, 0.0)
        rows = pl.ds(7, rim)
        for b in range(nb):
            eb[0, i, b, rows, :] = factor * (dy(2, b) - dz(1, b))
            eb[1, i, b, rows, :] = factor * (dz(0, b) - dx(2, b))
            eb[2, i, b, rows, :] = factor * (dx(1, b) - dy(0, b))
        return 0

    def relax_plane(i, _):
        mid, dx, dy, dz = differ(eb, (0, 1, 2), i, 8, cz, lane_core)
        for b in range(nb):
            B = [mid[c][b] for c in range(3)]
            J = [dy(2, b) - dz(1, b), dz(0, b) - dx(2, b), dx(1, b) - dy(0, b)]
            inv = (0.5 * time_step) / (drag * jnp.maximum(dot(B, B), 1.0))
            v = [u * inv for u in cross(J, B)]
            w = cross(v, B)
            for c in range(3):
                pot[c, i, b, core, :] = pot[c, i, b, core, :] + w[c]
        return 0

    for s in range(RELAX):
        r = DESCENTS + s
        send_halo(r, pot)
        take_halo(r, pot, pot, None)
        lax.fori_loop(1, cx + 3, induced_plane, 0)
        lax.fori_loop(2, cx + 2, relax_plane, 0)

    for b in range(nb):
        out_copy(pot, out_p, b, 1).start()
    for k, (src, out) in enumerate(((fld, out_r), (pot, out_p))):
        for b in range(nb):
            out_copy(src, out, b, k).wait()


def body(magnetic, friction):
    _, cx, cz, ny = magnetic.shape
    gxn, gzn = lax.axis_size("gx"), lax.axis_size("gz")
    nb = ny // LANES
    n = gxn * gzn
    full = (cx + 4, nb, cz + 16, LANES)
    VM = lambda *shape: pltpu.VMEM(shape, jnp.float32)
    DMA = lambda *shape: pltpu.SemaphoreType.DMA(shape)
    shape = jax.ShapeDtypeStruct(magnetic.shape, jnp.float32)
    return pl.pallas_call(
        functools.partial(kernel, gxn, gzn, cx, cz, nb),
        out_shape=(shape, shape),
        in_specs=[pl.BlockSpec(memory_space=pl.ANY), pl.BlockSpec(memory_space=pltpu.SMEM)],
        out_specs=(pl.BlockSpec(memory_space=pl.ANY), pl.BlockSpec(memory_space=pl.ANY)),
        scratch_shapes=[
            VM(3, *full), VM(3, *full), VM(3, *full), VM(4, *full),
            VM(ROUNDS, 2, 3, 2, nb, cz, LANES),
            VM(ROUNDS, 2, 3, cx, 2 * nb, LANES), VM(ROUNDS, 2, 3, cx, 2 * nb, LANES),
            VM(ROUNDS, 4, 3, nb, LANES), VM(ROUNDS, 4, 3, nb, LANES),
            VM(DESCENTS, 2, LANES), VM(DESCENTS, n, 2, LANES),
            VM(2, cx, nb, LANES), VM(gzn, 2, cx, nb, LANES), VM(2, cx, nb, LANES),
            DMA(ROUNDS, 8), DMA(ROUNDS, 8),
            DMA(DESCENTS, n), DMA(DESCENTS, n), DMA(gzn), DMA(gzn), DMA(nb), DMA(2, nb),
        ],
        compiler_params=pltpu.CompilerParams(
            collective_id=0, has_side_effects=True, vmem_limit_bytes=48 * 1024 * 1024
        ),
    )(magnetic, friction)


def solution(mesh):
    return jax.shard_map(
        body,
        mesh=mesh,
        in_specs=(P(None, "gx", "gz", "runs"), P("gz")),
        out_specs=(P(None, "gx", "gz", "runs"), P(None, "gx", "gz", "runs")),
        check_vma=False,
    )
```

profile of v0, /device:TPU:1, one launch (start us, length us, event | category | flops | bytes accessed | tf_op | source)
XLA Modules:
  0.0 68.7 jit_solution(7643266236064731478)
XLA Ops:
  0.6 0.0 copy-start
  0.6 1.4 %copy-done = f32[3,16,16,512]{3,2,1,0:T(8,128)S(1)} copy-done((f32[3,16,16,512]{3,2,1,0:T(8,128)S(1)}, f32[3,16,16,512]{3,2,1,0:T(8,128)}, u32[]{:S(2)}) %copy-start) | copy-done | bytes 1572888
  2.0 0.0 copy-start.1
  2.0 0.7 copy-done.1
  2.7 63.7 %shard_map.41 = (f32[3,16,16,512]{3,2,1,0:T(8,128)S(1)}, f32[3,16,16,512]{3,2,1,0:T(8,128)S(1)}) custom-call(f32[3,16,16,512]{3,2,1,0:T(8,128)S(1)} %copy-done, f32[16]{0:T(128)S(1)} %copy-done.1), custom_call_target="tpu_custom_call" | custom-call | tf_op jit(solution)/shard_map/pallas_call | solution.py:415
  66.4 1.1 %copy.6 = f32[3,16,16,512]{3,2,1,0:T(8,128)} copy(f32[3,16,16,512]{3,2,1,0:T(8,128)S(1)} %get-tuple-element.4) | data formatting | bytes 3145728
  67.6 1.1 %copy.7 = f32[3,16,16,512]{3,2,1,0:T(8,128)} copy(f32[3,16,16,512]{3,2,1,0:T(8,128)S(1)} %get-tuple-element.5) | data formatting | bytes 3145728
Async XLA Ops:
  0.6 1.4 %copy-start = (f32[3,16,16,512]{3,2,1,0:T(8,128)S(1)}, f32[3,16,16,512]{3,2,1,0:T(8,128)}, u32[]{:S(2)}) copy-start(f32[3,16,16,512]{3,2,1,0:T(8,128)} %mag.1) | copy-start | bytes 4718596
  2.0 0.7 copy-start.1
where the time goes:
time: 69.2 us; the launch traced here: 68.7 us
  Pallas kernels  63.7 us (92%)
  local copies, waits for them, and re-layouts  4.34 us (6%)
    pallas_call x1, Pallas kernels, body(): pl.pallas_call(functools.partial(kernel, gxn, gzn, cx, cz, nb), out_shape...  63.7 us
    unnamed x6, local copies, waits for them, and re-layouts  4.34 us

commit v1 on v0

--- a/solution.py
+++ b/solution.py
@@ -16,6 +16,8 @@
 time_step = 0.2
 
 DIRS = ((-1, 0), (1, 0), (0, -1), (0, 1), (-1, -1), (-1, 1), (1, -1), (1, 1))
+PARTS = ((((0, 3, True),),) * DESCENTS + (((1, 2, True), (0, 1, False)),) + (((1, 3, True), (0, 1, False)),) * (RELAX - 1))
+ZCOMPS = (3,) * DESCENTS + (2,) + (3,) * (RELAX - 1)
 OPP = (1, 0, 3, 2, 7, 6, 5, 4)
 
 
@@ -29,8 +31,8 @@
 
 def kernel(
     gxn, gzn, cx, cz, nb, mag, fric, out_r, out_p,
-    fld, pot, fb, eb, xr, zs, zr, cs, cr, ps, pr, ts, tr, above,
-    ssem, rsem, psend, precv, tsend, trecv, insem, osem,
+    fld, pot, fb, fb2, eb, xr, zs, zr, cs, cr, ps, pr, ts, tr, above,
+    xsend, xrecv, ssem, rsem, psend, precv, tsend, trecv, insem, osem,
 ):
     gx = lax.axis_index("gx")
     gz = lax.axis_index("gz")
@@ -90,14 +92,27 @@
             tests.append(gz > 0 if dz < 0 else gz < gzn - 1)
         return functools.reduce(jnp.logical_and, tests)
 
-    def link(r, d, src):
+    def near(side):
+        return 1 if side == 0 else 0
+
+    def x_link(r, d, q, src, arriving):
+        c0, c1, both = PARTS[r][q]
+        slot = d if arriving else OPP[d]
+        start = (2 if d == 0 else cx) + (0 if both else near(OPP[d]))
+        first, count = (0, 2) if both else (near(slot), 1)
+        return pltpu.make_async_remote_copy(
+            src_ref=src.at[pl.ds(c0, c1 - c0), pl.ds(start, count), :, core, :],
+            dst_ref=xr.at[r, slot, pl.ds(c0, c1 - c0), pl.ds(first, count)],
+            send_sem=xsend.at[r, d, q], recv_sem=xrecv.at[r, slot, q],
+            device_id={"gz": gz, "gx": gx + DIRS[d][0]}, device_id_type=pl.DeviceIdType.MESH,
+        )
+
+    def link(r, d, arriving):
         dx, dz = DIRS[d]
-        o = OPP[d]
-        if d < 2:
-            start = 2 if d == 0 else cx
-            s, t = src.at[:, pl.ds(start, 2), :, core, :], xr.at[r, o]
-        elif d < 4:
-            s, t = zs.at[r, d - 2], zr.at[r, o - 2]
+        o = d if arriving else OPP[d]
+        if d < 4:
+            comps = pl.ds(0, ZCOMPS[r])
+            s, t = zs.at[r, d - 2, comps], zr.at[r, o - 2, comps]
         else:
             s, t = cs.at[r, d - 4], cr.at[r, o - 4]
         return pltpu.make_async_remote_copy(
@@ -105,33 +120,20 @@
             device_id={"gz": gz + dz, "gx": gx + dx}, device_id_type=pl.DeviceIdType.MESH,
         )
 
-    def arrival(r, d, src):
-        dx, dz = DIRS[d]
-        if d < 2:
-            s, t = src.at[:, pl.ds(2, 2), :, core, :], xr.at[r, d]
-        elif d < 4:
-            s, t = zs.at[r, d - 2], zr.at[r, d - 2]
-        else:
-            s, t = cs.at[r, d - 4], cr.at[r, d - 4]
-        return pltpu.make_async_remote_copy(
-            src_ref=s, dst_ref=t, send_sem=ssem.at[r, d], recv_sem=rsem.at[r, d],
-            device_id={"gz": gz + dz, "gx": gx + dx}, device_id_type=pl.DeviceIdType.MESH,
-        )
-
-    def send_halo(r, src):
+    def send_x(r, src):
         for d in (0, 1):
             @pl.when(exists(d))
             def _(d=d):
-                link(r, d, src).start()
-
-        def pack(i, _):
-            for c in range(3):
-                for b in range(nb):
-                    zs[r, 0, c, i, 2 * b : 2 * b + 2, :] = src[c, i + 2, b, 8:10, :]
-                    zs[r, 1, c, i, 2 * b : 2 * b + 2, :] = src[c, i + 2, b, cz + 6 : cz + 8, :]
-            return 0
-
-        lax.fori_loop(0, cx, pack, 0)
+                for q in range(len(PARTS[r])):
+                    x_link(r, d, q, src, False).start()
+
+    def pack_plane(r, i, src):
+        for c in range(ZCOMPS[r]):
+            for b in range(nb):
+                zs[r, 0, c, i - 2, 2 * b : 2 * b + 2, :] = src[c, i, b, 8:10, :]
+                zs[r, 1, c, i - 2, 2 * b : 2 * b + 2, :] = src[c, i, b, cz + 6 : cz + 8, :]
+
+    def send_corners(r, src):
         for d in range(4, 8):
             dx, dz = DIRS[d]
             i = 2 if dx < 0 else cx + 1
@@ -139,46 +141,82 @@
             for c in range(3):
                 for b in range(nb):
                     cs[r, d - 4, c, b : b + 1, :] = src[c, i, b, k : k + 1, :]
-        for d in range(2, 8):
+        for d in range(4, 8):
             @pl.when(exists(d))
             def _(d=d):
-                link(r, d, src).start()
-
-    def take_halo(r, src, dst, mu):
-        def put(old, new):
-            return new if mu is None else old + mu * new
-
-        for d in (2, 3, 4, 5, 6, 7, 0, 1):
+                link(r, d, False).start()
+
+    def send_z(r):
+        for d in (2, 3):
+            @pl.when(exists(d))
+            def _(d=d):
+                link(r, d, False).start()
+
+    def loop(low, high, do, unroll=1):
+        def step(i, _):
+            do(i)
+            return 0
+
+        lax.fori_loop(low, high, step, 0, unroll=unroll)
+
+    def put(old, new, mu):
+        return new if mu is None else old + mu * new
+
+    def take_z(r, dst, mu):
+        for d in (2, 3):
+            @pl.when(exists(d))
+            def _(d=d):
+                link(r, d, True).wait_recv()
+                row = 6 if d == 2 else cz + 8
+
+                def unpack(i):
+                    for c in range(ZCOMPS[r]):
+                        for b in range(nb):
+                            dst[c, i + 2, b, row : row + 2, :] = put(
+                                dst[c, i + 2, b, row : row + 2, :], zr[r, d - 2, c, i, 2 * b : 2 * b + 2, :], mu
+                            )
+
+                loop(0, cx, unpack, 2)
+                link(r, d, False).wait_send()
+
+    def take_x(r, src, dst, mu):
+        for d in (4, 5, 6, 7):
             dx, dz = DIRS[d]
 
             @pl.when(exists(d))
             def _(d=d, dx=dx, dz=dz):
-                arrival(r, d, src).wait_recv()
-                if d < 2:
-                    base = 0 if d == 0 else cx + 2
-                    for c in range(3):
-                        for p in range(2):
+                link(r, d, True).wait_recv()
+                i = 1 if dx < 0 else cx + 2
+                k = 7 if dz < 0 else cz + 8
+                for c in range(3):
+                    for b in range(nb):
+                        dst[c, i, b, k : k + 1, :] = put(dst[c, i, b, k : k + 1, :], cr[r, d - 4, c, b : b + 1, :], mu)
+                link(r, d, False).wait_send()
+
+        for d in (0, 1):
+            @pl.when(exists(d))
+            def _(d=d):
+                base = 0 if d == 0 else cx + 2
+                for q, (c0, c1, both) in enumerate(PARTS[r]):
+                    x_link(r, d, q, src, True).wait_recv()
+                    for c in range(c0, c1):
+                        for p in range(2) if both else (near(d),):
                             for b in range(nb):
-                                dst[c, base + p, b, core, :] = put(dst[c, base + p, b, core, :], xr[r, d, c, p, b])
-                elif d < 4:
-                    row = 6 if d == 2 else cz + 8
-
-                    def unpack(i, _):
-                        for c in range(3):
-                            for b in range(nb):
-                                dst[c, i + 2, b, row : row + 2, :] = put(
-                                    dst[c, i + 2, b, row : row + 2, :], zr[r, d - 2, c, i, 2 * b : 2 * b + 2, :]
+                                dst[c, base + p, b, core, :] = put(
+                                    dst[c, base + p, b, core, :], xr[r, d, c, p, b], mu
                                 )
-                        return 0
-
-                    lax.fori_loop(0, cx, unpack, 0)
-                else:
-                    i = 1 if dx < 0 else cx + 2
-                    k = 7 if dz < 0 else cz + 8
-                    for c in range(3):
-                        for b in range(nb):
-                            dst[c, i, b, k : k + 1, :] = put(dst[c, i, b, k : k + 1, :], cr[r, d - 4, c, b : b + 1, :])
-                link(r, d, src).wait_send()
+
+        for d in (0, 1):
+            @pl.when(exists(d))
+            def _(d=d):
+                for q in range(len(PARTS[r])):
+                    x_link(r, d, q, src, False).wait_send()
+
+    def over_edges(do, acc, low, width):
+        def step(j, acc):
+            return do(low + j + jnp.where(j >= width, cx + 3 - 2 * low - 2 * width + 1, 0), acc)
+
+        return lax.fori_loop(0, 2 * width, step, acc)
 
     def differ(ref, comps, i, r0, rows, lane):
         first, last = lane == 0, lane == LANES - 1
@@ -247,7 +285,7 @@
             ]
             F = [fb[c, i, b, core, :] + 0.5 * curl[c] for c in range(3)]
             for c in range(3):
-                fb[c, i, b, core, :] = F[c]
+                fb2[c, i, b, core, :] = F[c]
             acc = acc + folded(dot(F, F))
         return acc
 
@@ -285,26 +323,102 @@
         sums = jnp.sum(total, axis=1, keepdims=True) / (n * cx * cz * nb * LANES)
         return step_scale * sums[0:1] / (sums[1:2] + 1e-6)
 
-    send_halo(0, fld)
-    take_halo(0, fld, fld, None)
+    def suffix_plane(i, src, dst, slot):
+        for c, other, sign in ((0, 1, -1.0), (1, 0, 1.0)):
+            for b in range(nb):
+                v = sign * src[other, i, b, core, :]
+                step = 1
+                while step < cz:
+                    v = v + jnp.where(row_core < cz - step, pltpu.roll(v, cz - step, 0), 0.0)
+                    step *= 2
+                dst[c, i, b, core, :] = v
+                ts[slot, c, i - 2, b : b + 1, :] = v[0:1]
+
+    def column_copy(slot, k, dz):
+        return pltpu.make_async_remote_copy(
+            src_ref=ts.at[slot], dst_ref=tr.at[slot, k], send_sem=tsend.at[slot, k], recv_sem=trecv.at[slot, k],
+            device_id={"gz": gz + dz, "gx": gx}, device_id_type=pl.DeviceIdType.MESH,
+        )
+
+    def send_columns(slot):
+        for k in range(1, gzn):
+            @pl.when(gz - k >= 0)
+            def _(k=k):
+                column_copy(slot, k - 1, -k).start()
+
+    send_x(0, fld)
+    loop(2, cx + 2, lambda i: pack_plane(0, i, fld), 2)
+    send_z(0)
+    send_corners(0, fld)
     zero = jnp.zeros((8, LANES), f32)
+    mu = None
     for s in range(DESCENTS):
-        lsum = lax.fori_loop(1, cx + 3, omega_plane, zero)
-        gsum = lax.fori_loop(2, cx + 2, force_plane, zero)
+        last = s == DESCENTS - 1
+        take_z(s, fld, mu)
+        lsum = lax.fori_loop(3, cx + 1, omega_plane, zero)
+        take_x(s, fld if s == 0 else fb2, fld, mu)
+        lsum = over_edges(omega_plane, lsum, 1, 2)
+
+        def force(i, acc):
+            acc = force_plane(i, acc)
+            if not last:
+                pack_plane(s + 1, i, fb2)
+            return acc
+
+        gsum = over_edges(force, zero, 2, 2)
+        if not last:
+            send_x(s + 1, fb2)
+            send_corners(s + 1, fb2)
+        gsum = lax.fori_loop(4, cx, force, gsum)
         send_sums(s, lsum, gsum)
-        if s < DESCENTS - 1:
-            send_halo(s + 1, fb)
+        if not last:
+            send_z(s + 1)
+        else:
+            loop(2, cx + 2, lambda i: suffix_plane(i, fb2, eb, 1))
+            send_columns(1)
         mu = take_sums(s)
 
-        def update(i, _):
+        def update(i):
             for c in range(3):
                 for b in range(nb):
-                    fld[c, i, b, core, :] = fld[c, i, b, core, :] + mu * fb[c, i, b, core, :]
-            return 0
-
-        lax.fori_loop(2, cx + 2, update, 0)
-        if s < DESCENTS - 1:
-            take_halo(s + 1, fb, fld, mu)
+                    fld[c, i, b, core, :] = fld[c, i, b, core, :] + mu * fb2[c, i, b, core, :]
+
+        if not last:
+            loop(2, cx + 2, update)
+        if s == DESCENTS - 2:
+            loop(2, cx + 2, lambda i: suffix_plane(i, fld, pot, 0))
+            send_columns(0)
+
+    above[...] = jnp.zeros(above.shape, f32)
+    for k in range(1, gzn):
+        @pl.when(gz + k < gzn)
+        def _(k=k):
+            column_copy(0, k - 1, k).wait_recv()
+            column_copy(1, k - 1, k).wait_recv()
+
+            def gather(i):
+                for c in range(2):
+                    above[c, i] = above[c, i] + (tr[0, k - 1, c, i] + mu * tr[1, k - 1, c, i])
+
+            loop(0, cx, gather, 2)
+
+    def lift(i, acc):
+        for c in range(2):
+            for b in range(nb):
+                pot[c, i, b, core, :] = (pot[c, i, b, core, :] + mu * eb[c, i, b, core, :]) + above[
+                    c, i - 2, b : b + 1, :
+                ]
+        for b in range(nb):
+            pot[2, i, b, core, :] = jnp.zeros((cz, LANES), f32)
+        pack_plane(DESCENTS, i, pot)
+        return acc
+
+    over_edges(lift, 0, 2, 2)
+    send_x(DESCENTS, pot)
+    lax.fori_loop(4, cx, lift, 0)
+    send_z(DESCENTS)
+    send_corners(DESCENTS, pot)
+    loop(2, cx + 2, update)
 
     def out_copy(src, out, b, k):
         return pltpu.make_async_copy(
@@ -313,52 +427,11 @@
 
     for b in range(nb):
         out_copy(fld, out_r, b, 0).start()
-
-    def suffix_plane(i, _):
-        for c, other, sign in ((0, 1, -1.0), (1, 0, 1.0)):
-            for b in range(nb):
-                v = sign * fld[other, i, b, core, :]
-                step = 1
-                while step < cz:
-                    v = v + jnp.where(row_core < cz - step, pltpu.roll(v, cz - step, 0), 0.0)
-                    step *= 2
-                pot[c, i, b, core, :] = v
-                ts[c, i - 2, b : b + 1, :] = v[0:1]
-        for b in range(nb):
-            pot[2, i, b, core, :] = jnp.zeros((cz, LANES), f32)
-        return 0
-
-    lax.fori_loop(2, cx + 2, suffix_plane, 0)
-
-    def column_copy(k, dz):
-        return pltpu.make_async_remote_copy(
-            src_ref=ts, dst_ref=tr.at[k], send_sem=tsend.at[k], recv_sem=trecv.at[k],
-            device_id={"gz": gz + dz, "gx": gx}, device_id_type=pl.DeviceIdType.MESH,
-        )
-
-    for k in range(1, gzn):
-        @pl.when(gz - k >= 0)
-        def _(k=k):
-            column_copy(k - 1, -k).start()
-
-    above[...] = jnp.zeros(above.shape, f32)
-    for k in range(1, gzn):
-        @pl.when(gz + k < gzn)
-        def _(k=k):
-            column_copy(k - 1, k).wait_recv()
-            above[...] = above[...] + tr[k - 1]
-
-    def lift(i, _):
-        for c in range(2):
-            for b in range(nb):
-                pot[c, i, b, core, :] = pot[c, i, b, core, :] + above[c, i - 2, b : b + 1, :]
-        return 0
-
-    lax.fori_loop(2, cx + 2, lift, 0)
-    for k in range(1, gzn):
-        @pl.when(gz - k >= 0)
-        def _(k=k):
-            column_copy(k - 1, -k).wait_send()
+    for slot in range(2):
+        for k in range(1, gzn):
+            @pl.when(gz - k >= 0)
+            def _(slot=slot, k=k):
+                column_copy(slot, k - 1, -k).wait_send()
 
     drag = jnp.zeros((cz, LANES), f32)
     for k in range(cz):
@@ -366,7 +439,7 @@
     z_at = gz * cz + row_rim - 1
     z_in = (z_at >= 0) & (z_at < gzn * cz)
 
-    def induced_plane(i, _):
+    def induced_plane(i, acc):
         mid, dx, dy, dz = differ(pot, (0, 1, 2), i, 7, rim, lane_rim)
         x_at = gx * cx + i - 2
         factor = jnp.where(z_in & ((x_at >= 0) & (x_at < gxn * cx)), 0.5, 0.0)
@@ -375,9 +448,9 @@
             eb[0, i, b, rows, :] = factor * (dy(2, b) - dz(1, b))
             eb[1, i, b, rows, :] = factor * (dz(0, b) - dx(2, b))
             eb[2, i, b, rows, :] = factor * (dx(1, b) - dy(0, b))
-        return 0
-
-    def relax_plane(i, _):
+        return acc
+
+    def relax_plane(i):
         mid, dx, dy, dz = differ(eb, (0, 1, 2), i, 8, cz, lane_core)
         for b in range(nb):
             B = [mid[c][b] for c in range(3)]
@@ -387,14 +460,29 @@
             w = cross(v, B)
             for c in range(3):
                 pot[c, i, b, core, :] = pot[c, i, b, core, :] + w[c]
-        return 0
 
     for s in range(RELAX):
         r = DESCENTS + s
-        send_halo(r, pot)
-        take_halo(r, pot, pot, None)
-        lax.fori_loop(1, cx + 3, induced_plane, 0)
-        lax.fori_loop(2, cx + 2, relax_plane, 0)
+        last = s == RELAX - 1
+        take_z(r, pot, None)
+        lax.fori_loop(3, cx + 1, induced_plane, 0)
+        take_x(r, pot, pot, None)
+        over_edges(induced_plane, 0, 1, 2)
+
+        def relax(i, acc):
+            relax_plane(i)
+            if not last:
+                pack_plane(r + 1, i, pot)
+            return acc
+
+        if last:
+            lax.fori_loop(2, cx + 2, relax, 0)
+        else:
+            over_edges(relax, 0, 2, 2)
+            send_x(r + 1, pot)
+            send_corners(r + 1, pot)
+            lax.fori_loop(4, cx, relax, 0)
+            send_z(r + 1)
 
     for b in range(nb):
         out_copy(pot, out_p, b, 1).start()
@@ -415,17 +503,18 @@
     return pl.pallas_call(
         functools.partial(kernel, gxn, gzn, cx, cz, nb),
         out_shape=(shape, shape),
-        in_specs=[pl.BlockSpec(memory_space=pl.ANY), pl.BlockSpec(memory_space=pltpu.SMEM)],
+        in_specs=[pl.BlockSpec(memory_space=pltpu.HBM), pl.BlockSpec(memory_space=pltpu.SMEM)],
         out_specs=(pl.BlockSpec(memory_space=pl.ANY), pl.BlockSpec(memory_space=pl.ANY)),
         scratch_shapes=[
-            VM(3, *full), VM(3, *full), VM(3, *full), VM(4, *full),
+            VM(3, *full), VM(3, *full), VM(3, *full), VM(3, *full), VM(4, *full),
             VM(ROUNDS, 2, 3, 2, nb, cz, LANES),
             VM(ROUNDS, 2, 3, cx, 2 * nb, LANES), VM(ROUNDS, 2, 3, cx, 2 * nb, LANES),
             VM(ROUNDS, 4, 3, nb, LANES), VM(ROUNDS, 4, 3, nb, LANES),
             VM(DESCENTS, 2, LANES), VM(DESCENTS, n, 2, LANES),
-            VM(2, cx, nb, LANES), VM(gzn, 2, cx, nb, LANES), VM(2, cx, nb, LANES),
+            VM(2, 2, cx, nb, LANES), VM(2, gzn, 2, cx, nb, LANES), VM(2, cx, nb, LANES),
+            DMA(ROUNDS, 2, 2), DMA(ROUNDS, 2, 2),
             DMA(ROUNDS, 8), DMA(ROUNDS, 8),
-            DMA(DESCENTS, n), DMA(DESCENTS, n), DMA(gzn), DMA(gzn), DMA(nb), DMA(2, nb),
+            DMA(DESCENTS, n), DMA(DESCENTS, n), DMA(2, gzn), DMA(2, gzn), DMA(nb), DMA(2, nb),
         ],
         compiler_params=pltpu.CompilerParams(
             collective_id=0, has_side_effects=True, vmem_limit_bytes=48 * 1024 * 1024

time: 69.2 us -> 59.7 us (0.86)
  Pallas kernels: 63.7 us -> 54.5 us
    pallas_call x1, Pallas kernels: 63.7 us -> 54.5 us  [body(): pl.pallas_call(functools.partial(kernel, gxn, gzn, cx, cz, nb), out_shape...]
where the time goes in v1:
time: 59.7 us; the launch traced here: 59.5 us
  Pallas kernels  54.5 us (91%)
  local copies, waits for them, and re-layouts  4.34 us (7%)
  between operations  0.65 us (1%)
    pallas_call x1, Pallas kernels, body(): pl.pallas_call(functools.partial(kernel, gxn, gzn, cx, cz, nb), out_shape...  54.5 us
    unnamed x6, local copies, waits for them, and re-layouts  4.34 us

profile of v1, /device:TPU:1, one launch (start us, length us, event | category | flops | bytes accessed | tf_op | source)
XLA Modules:
  0.0 59.5 jit_solution(17467295726600171050)
XLA Ops:
  0.6 0.0 copy-start
  0.6 1.4 %copy-done = f32[3,16,16,512]{3,2,1,0:T(8,128)S(1)} copy-done((f32[3,16,16,512]{3,2,1,0:T(8,128)S(1)}, f32[3,16,16,512]{3,2,1,0:T(8,128)}, u32[]{:S(2)}) %copy-start) | copy-done | bytes 1572888
  2.0 0.0 copy-start.1
  2.0 0.7 %copy-done.1 = f32[16]{0:T(128)S(1)} copy-done((f32[16]{0:T(128)S(1)}, f32[16]{0:T(128)}, u32[]{:S(2)}) %copy-start.1) | copy-done | bytes 88
  2.7 54.5 %shard_map.41 = (f32[3,16,16,512]{3,2,1,0:T(8,128)S(1)}, f32[3,16,16,512]{3,2,1,0:T(8,128)S(1)}) custom-call(f32[3,16,16,512]{3,2,1,0:T(8,128)S(1)} %copy-done, f32[16]{0:T(128)S(1)} %copy-done.1), custom_call_target="tpu_custom_call" | custom-call | tf_op jit(solution)/shard_map/pallas_call | solution.py:503
  57.2 1.1 %copy.6 = f32[3,16,16,512]{3,2,1,0:T(8,128)} copy(f32[3,16,16,512]{3,2,1,0:T(8,128)S(1)} %get-tuple-element.4) | data formatting | bytes 3145728
  58.4 1.1 %copy.7 = f32[3,16,16,512]{3,2,1,0:T(8,128)} copy(f32[3,16,16,512]{3,2,1,0:T(8,128)S(1)} %get-tuple-element.5) | data formatting | bytes 3145728
Async XLA Ops:
  0.6 1.4 %copy-start = (f32[3,16,16,512]{3,2,1,0:T(8,128)S(1)}, f32[3,16,16,512]{3,2,1,0:T(8,128)}, u32[]{:S(2)}) copy-start(f32[3,16,16,512]{3,2,1,0:T(8,128)} %mag.1) | copy-start | bytes 4718596
  2.0 0.7 %copy-start.1 = (f32[16]{0:T(128)S(1)}, f32[16]{0:T(128)}, u32[]{:S(2)}) copy-start(f32[16]{0:T(128)} %fric.1) | copy-start | bytes 196

commit v2 on v1

--- a/solution.py
+++ b/solution.py
@@ -79,7 +79,6 @@
 
         lax.fori_loop(2, cx + 2, clear, 0)
 
-    pl.semaphore_wait(barrier, n - 1)
     for b in range(nb):
         in_copy(b).wait()
 
@@ -133,7 +132,7 @@
                 zs[r, 0, c, i - 2, 2 * b : 2 * b + 2, :] = src[c, i, b, 8:10, :]
                 zs[r, 1, c, i - 2, 2 * b : 2 * b + 2, :] = src[c, i, b, cz + 6 : cz + 8, :]
 
-    def send_corners(r, src):
+    def pack_corners(r, src):
         for d in range(4, 8):
             dx, dz = DIRS[d]
             i = 2 if dx < 0 else cx + 1
@@ -141,6 +140,8 @@
             for c in range(3):
                 for b in range(nb):
                     cs[r, d - 4, c, b : b + 1, :] = src[c, i, b, k : k + 1, :]
+
+    def send_corners(r):
         for d in range(4, 8):
             @pl.when(exists(d))
             def _(d=d):
@@ -323,7 +324,7 @@
         sums = jnp.sum(total, axis=1, keepdims=True) / (n * cx * cz * nb * LANES)
         return step_scale * sums[0:1] / (sums[1:2] + 1e-6)
 
-    def suffix_plane(i, src, dst, slot):
+    def suffix_plane(i, src, dst):
         for c, other, sign in ((0, 1, -1.0), (1, 0, 1.0)):
             for b in range(nb):
                 v = sign * src[other, i, b, core, :]
@@ -332,7 +333,11 @@
                     v = v + jnp.where(row_core < cz - step, pltpu.roll(v, cz - step, 0), 0.0)
                     step *= 2
                 dst[c, i, b, core, :] = v
-                ts[slot, c, i - 2, b : b + 1, :] = v[0:1]
+
+    def column_plane(i, src, slot):
+        for c in range(2):
+            for b in range(nb):
+                ts[slot, c, i - 2, b : b + 1, :] = src[c, i, b, 8:9, :]
 
     def column_copy(slot, k, dz):
         return pltpu.make_async_remote_copy(
@@ -346,10 +351,13 @@
             def _(k=k):
                 column_copy(slot, k - 1, -k).start()
 
+    loop(2, cx + 2, lambda i: pack_plane(0, i, fld), 2)
+    pack_corners(0, fld)
+    pl.semaphore_wait(barrier, n - 1)
     send_x(0, fld)
-    loop(2, cx + 2, lambda i: pack_plane(0, i, fld), 2)
     send_z(0)
-    send_corners(0, fld)
+    send_corners(0)
+    loop(2, cx + 2, lambda i: suffix_plane(i, fld, pot))
     zero = jnp.zeros((8, LANES), f32)
     mu = None
     for s in range(DESCENTS):
@@ -368,13 +376,15 @@
         gsum = over_edges(force, zero, 2, 2)
         if not last:
             send_x(s + 1, fb2)
-            send_corners(s + 1, fb2)
+            pack_corners(s + 1, fb2)
+            send_corners(s + 1)
         gsum = lax.fori_loop(4, cx, force, gsum)
         send_sums(s, lsum, gsum)
         if not last:
             send_z(s + 1)
-        else:
-            loop(2, cx + 2, lambda i: suffix_plane(i, fb2, eb, 1))
+        loop(2, cx + 2, lambda i: suffix_plane(i, fb2, eb))
+        if last:
+            loop(2, cx + 2, lambda i: column_plane(i, eb, 1), 2)
             send_columns(1)
         mu = take_sums(s)
 
@@ -383,10 +393,16 @@
                 for b in range(nb):
                     fld[c, i, b, core, :] = fld[c, i, b, core, :] + mu * fb2[c, i, b, core, :]
 
+        def advance(i):
+            update(i)
+            for c in range(2):
+                for b in range(nb):
+                    pot[c, i, b, core, :] = pot[c, i, b, core, :] + mu * eb[c, i, b, core, :]
+            column_plane(i, pot, 0)
+
         if not last:
-            loop(2, cx + 2, update)
+            loop(2, cx + 2, advance)
         if s == DESCENTS - 2:
-            loop(2, cx + 2, lambda i: suffix_plane(i, fld, pot, 0))
             send_columns(0)
 
     above[...] = jnp.zeros(above.shape, f32)
@@ -417,7 +433,8 @@
     send_x(DESCENTS, pot)
     lax.fori_loop(4, cx, lift, 0)
     send_z(DESCENTS)
-    send_corners(DESCENTS, pot)
+    pack_corners(DESCENTS, pot)
+    send_corners(DESCENTS)
     loop(2, cx + 2, update)
 
     def out_copy(src, out, b, k):
@@ -480,7 +497,8 @@
         else:
             over_edges(relax, 0, 2, 2)
             send_x(r + 1, pot)
-            send_corners(r + 1, pot)
+            pack_corners(r + 1, pot)
+            send_corners(r + 1)
             lax.fori_loop(4, cx, relax, 0)
             send_z(r + 1)
 
@@ -517,7 +535,7 @@
             DMA(DESCENTS, n), DMA(DESCENTS, n), DMA(2, gzn), DMA(2, gzn), DMA(nb), DMA(2, nb),
         ],
         compiler_params=pltpu.CompilerParams(
-            collective_id=0, has_side_effects=True, vmem_limit_bytes=48 * 1024 * 1024
+            collective_id=0, has_side_effects=True, vmem_limit_bytes=67043328
         ),
     )(magnetic, friction)
 

time: 59.7 us -> 60 us (level)
  Pallas kernels: 54.5 us -> 55.1 us
    pallas_call x1, Pallas kernels: 54.5 us -> 55.1 us  [body(): pl.pallas_call(functools.partial(kernel, gxn, gzn, cx, cz, nb), out_shape...]
    unnamed x6 -> x4, local copies, waits for them, and re-layouts: 4.34 us -> 4.03 us
where the time goes in v2:
time: 60 us; the launch traced here: 59.8 us
  Pallas kernels  55.1 us (92%)
  local copies, waits for them, and re-layouts  4.03 us (7%)
  between operations  0.65 us (1%)
    pallas_call x1, Pallas kernels, body(): pl.pallas_call(functools.partial(kernel, gxn, gzn, cx, cz, nb), out_shape...  55.1 us
    unnamed x4, local copies, waits for them, and re-layouts  4.03 us

profile of v2, /device:TPU:1, one launch (start us, length us, event | category | flops | bytes accessed | tf_op | source)
XLA Modules:
  0.0 59.8 jit_solution(1002205990891230949)
XLA Ops:
  0.6 55.1 %shard_map.41 = (f32[3,16,16,512]{3,2,1,0:T(8,128)}, f32[3,16,16,512]{3,2,1,0:T(8,128)}) custom-call(f32[3,16,16,512]{3,2,1,0:T(8,128)} %mag.1, f32[16]{0:T(128)} %fric.1), custom_call_target="tpu_custom_call" | custom-call | tf_op jit(solution)/shard_map/pallas_call | solution.py:521
  55.8 0.0 copy-start
  55.8 2.9 %copy.6 = f32[3,16,16,512]{3,2,1,0:T(8,128)} copy(f32[3,16,16,512]{3,2,1,0:T(8,128)} %get-tuple-element.4) | data formatting | bytes 3145728
  58.7 0.0 copy-done
  58.7 1.1 %copy.7 = f32[3,16,16,512]{3,2,1,0:T(8,128)} copy(f32[3,16,16,512]{3,2,1,0:T(8,128)S(1)} %copy-done) | data formatting | bytes 3145728
Async XLA Ops:
  55.8 2.9 %copy-start = (f32[3,16,16,512]{3,2,1,0:T(8,128)S(1)}, f32[3,16,16,512]{3,2,1,0:T(8,128)}, u32[]{:S(2)}) copy-start(f32[3,16,16,512]{3,2,1,0:T(8,128)} %get-tuple-element.5) | copy-start | bytes 4718596

commit v3 on v2

--- a/solution.py
+++ b/solution.py
@@ -262,27 +262,31 @@
                 0.5 * (dx(1, b) - dy(0, b)),
             ]
             D = 0.5 * (dx(0, b) + dy(1, b) + dz(2, b))
-            inv = 1.0 / jnp.maximum(dot(B, B), 1.0)
+            square = dot(B, B)
+            inv = 1.0 / jnp.maximum(square, 1.0)
+            part = square * inv
             L = cross(J, B)
-            om = [(L[c] - D * B[c]) * inv for c in range(3)]
-            E = cross(om, B)
+            Li = [u * inv for u in L]
+            E = cross(Li, B)
             for c in range(3):
                 eb[c, i, b, rows, :] = E[c]
-            eb[3, i, b, rows, :] = dot(om, B)
-            oj = cross(om, J)
-            oo = dot(om, om)
-            for c in range(3):
-                fb[c, i, b, rows, :] = om[c] * D - oj[c] + oo * B[c]
-            acc = acc + folded(jnp.where(inner, dot(L, L) * inv + D * D, 0.0))
+            eb[3, i, b, rows, :] = D * part
+            drive = dot(L, Li)
+            dd = D * D
+            scale = inv * (drive + (dd * part - dd))
+            lj = cross(Li, J)
+            for c in range(3):
+                fb[c, i, b, rows, :] = scale * B[c] - lj[c]
+            acc = acc + folded(jnp.where(inner, drive + dd, 0.0))
         return acc
 
     def force_plane(i, acc):
         mid, dx, dy, dz = differ(eb, (0, 1, 2, 3), i, 8, cz, lane_core)
         for b in range(nb):
             curl = [
-                dy(2, b) - dz(1, b) - dx(3, b),
-                dz(0, b) - dx(2, b) - dy(3, b),
-                dx(1, b) - dy(0, b) - dz(3, b),
+                dy(2, b) - dz(1, b) + dx(3, b),
+                dz(0, b) - dx(2, b) + dy(3, b),
+                dx(1, b) - dy(0, b) + dz(3, b),
             ]
             F = [fb[c, i, b, core, :] + 0.5 * curl[c] for c in range(3)]
             for c in range(3):
@@ -535,7 +539,7 @@
             DMA(DESCENTS, n), DMA(DESCENTS, n), DMA(2, gzn), DMA(2, gzn), DMA(nb), DMA(2, nb),
         ],
         compiler_params=pltpu.CompilerParams(
-            collective_id=0, has_side_effects=True, vmem_limit_bytes=67043328
+            collective_id=0, has_side_effects=True, vmem_limit_bytes=48 * 1024 * 1024
         ),
     )(magnetic, friction)
 

time: 60 us -> 58.6 us (0.977)
  Pallas kernels: 55.1 us -> 53.5 us
    pallas_call x1, Pallas kernels: 55.1 us -> 53.5 us  [body(): pl.pallas_call(functools.partial(kernel, gxn, gzn, cx, cz, nb), out_shape...]
    unnamed x4 -> x6, local copies, waits for them, and re-layouts: 4.03 us -> 4.34 us
where the time goes in v3:
time: 58.6 us; the launch traced here: 58.5 us
  Pallas kernels  53.5 us (91%)
  local copies, waits for them, and re-layouts  4.34 us (7%)
  between operations  0.65 us (1%)
    pallas_call x1, Pallas kernels, body(): pl.pallas_call(functools.partial(kernel, gxn, gzn, cx, cz, nb), out_shape...  53.5 us
    unnamed x6, local copies, waits for them, and re-layouts  4.34 us

profile of v3, /device:TPU:1, one launch (start us, length us, event | category | flops | bytes accessed | tf_op | source)
XLA Modules:
  0.0 58.5 jit_solution(8797159827372228601)
XLA Ops:
  0.6 0.0 copy-start
  0.6 1.4 %copy-done = f32[3,16,16,512]{3,2,1,0:T(8,128)S(1)} copy-done((f32[3,16,16,512]{3,2,1,0:T(8,128)S(1)}, f32[3,16,16,512]{3,2,1,0:T(8,128)}, u32[]{:S(2)}) %copy-start) | copy-done | bytes 1572888
  2.0 0.0 copy-start.1
  2.0 0.7 %copy-done.1 = f32[16]{0:T(128)S(1)} copy-done((f32[16]{0:T(128)S(1)}, f32[16]{0:T(128)}, u32[]{:S(2)}) %copy-start.1) | copy-done | bytes 88
  2.7 53.5 %shard_map.41 = (f32[3,16,16,512]{3,2,1,0:T(8,128)S(1)}, f32[3,16,16,512]{3,2,1,0:T(8,128)S(1)}) custom-call(f32[3,16,16,512]{3,2,1,0:T(8,128)S(1)} %copy-done, f32[16]{0:T(128)S(1)} %copy-done.1), custom_call_target="tpu_custom_call" | custom-call | tf_op jit(solution)/shard_map/pallas_call | solution.py:525
  56.2 1.1 %copy.6 = f32[3,16,16,512]{3,2,1,0:T(8,128)} copy(f32[3,16,16,512]{3,2,1,0:T(8,128)S(1)} %get-tuple-element.4) | data formatting | bytes 3145728
  57.3 1.1 %copy.7 = f32[3,16,16,512]{3,2,1,0:T(8,128)} copy(f32[3,16,16,512]{3,2,1,0:T(8,128)S(1)} %get-tuple-element.5) | data formatting | bytes 3145728
Async XLA Ops:
  0.6 1.4 %copy-start = (f32[3,16,16,512]{3,2,1,0:T(8,128)S(1)}, f32[3,16,16,512]{3,2,1,0:T(8,128)}, u32[]{:S(2)}) copy-start(f32[3,16,16,512]{3,2,1,0:T(8,128)} %mag.1) | copy-start | bytes 4718596
  2.0 0.7 %copy-start.1 = (f32[16]{0:T(128)S(1)}, f32[16]{0:T(128)}, u32[]{:S(2)}) copy-start(f32[16]{0:T(128)} %fric.1) | copy-start | bytes 196

commit v4 on v3

--- a/solution.py
+++ b/solution.py
@@ -32,7 +32,7 @@
 def kernel(
     gxn, gzn, cx, cz, nb, mag, fric, out_r, out_p,
     fld, pot, fb, fb2, eb, xr, zs, zr, cs, cr, ps, pr, ts, tr, above,
-    xsend, xrecv, ssem, rsem, psend, precv, tsend, trecv, insem, osem,
+    xsend, xrecv, zsend, zrecv, ssem, rsem, psend, precv, tsend, trecv, insem, osem,
 ):
     gx = lax.axis_index("gx")
     gz = lax.axis_index("gz")
@@ -106,16 +106,22 @@
             device_id={"gz": gz, "gx": gx + DIRS[d][0]}, device_id_type=pl.DeviceIdType.MESH,
         )
 
+    half = cx // 2
+
+    def z_link(r, d, h, arriving):
+        o = d if arriving else OPP[d]
+        comps, planes = pl.ds(0, ZCOMPS[r]), pl.ds(h * half, half)
+        return pltpu.make_async_remote_copy(
+            src_ref=zs.at[r, d - 2, comps, planes], dst_ref=zr.at[r, o - 2, comps, planes],
+            send_sem=zsend.at[r, d - 2, h], recv_sem=zrecv.at[r, o - 2, h],
+            device_id={"gz": gz + DIRS[d][1], "gx": gx}, device_id_type=pl.DeviceIdType.MESH,
+        )
+
     def link(r, d, arriving):
         dx, dz = DIRS[d]
         o = d if arriving else OPP[d]
-        if d < 4:
-            comps = pl.ds(0, ZCOMPS[r])
-            s, t = zs.at[r, d - 2, comps], zr.at[r, o - 2, comps]
-        else:
-            s, t = cs.at[r, d - 4], cr.at[r, o - 4]
         return pltpu.make_async_remote_copy(
-            src_ref=s, dst_ref=t, send_sem=ssem.at[r, d], recv_sem=rsem.at[r, o],
+            src_ref=cs.at[r, d - 4], dst_ref=cr.at[r, o - 4], send_sem=ssem.at[r, d], recv_sem=rsem.at[r, o],
             device_id={"gz": gz + dz, "gx": gx + dx}, device_id_type=pl.DeviceIdType.MESH,
         )
 
@@ -147,11 +153,11 @@
             def _(d=d):
                 link(r, d, False).start()
 
-    def send_z(r):
+    def send_z(r, h):
         for d in (2, 3):
             @pl.when(exists(d))
             def _(d=d):
-                link(r, d, False).start()
+                z_link(r, d, h, False).start()
 
     def loop(low, high, do, unroll=1):
         def step(i, _):
@@ -163,11 +169,11 @@
     def put(old, new, mu):
         return new if mu is None else old + mu * new
 
-    def take_z(r, dst, mu):
+    def take_z(r, dst, mu, h):
         for d in (2, 3):
             @pl.when(exists(d))
             def _(d=d):
-                link(r, d, True).wait_recv()
+                z_link(r, d, h, True).wait_recv()
                 row = 6 if d == 2 else cz + 8
 
                 def unpack(i):
@@ -177,8 +183,22 @@
                                 dst[c, i + 2, b, row : row + 2, :], zr[r, d - 2, c, i, 2 * b : 2 * b + 2, :], mu
                             )
 
-                loop(0, cx, unpack, 2)
-                link(r, d, False).wait_send()
+                loop(h * half, h * half + half, unpack, 2)
+                z_link(r, d, h, False).wait_send()
+
+    def inner_planes(r, dst, mu, do, acc):
+        for h in range(2):
+            take_z(r, dst, mu, h)
+            low, high = (3, half + 1) if h == 0 else (half + 1, cx + 1)
+            acc = lax.fori_loop(low, high, do, acc)
+        return acc
+
+    def later_planes(r, do, acc):
+        acc = lax.fori_loop(4, half + 2, do, acc)
+        send_z(r, 0)
+        acc = lax.fori_loop(half + 2, cx, do, acc)
+        send_z(r, 1)
+        return acc
 
     def take_x(r, src, dst, mu):
         for d in (4, 5, 6, 7):
@@ -359,15 +379,15 @@
     pack_corners(0, fld)
     pl.semaphore_wait(barrier, n - 1)
     send_x(0, fld)
-    send_z(0)
+    send_z(0, 0)
+    send_z(0, 1)
     send_corners(0)
     loop(2, cx + 2, lambda i: suffix_plane(i, fld, pot))
     zero = jnp.zeros((8, LANES), f32)
     mu = None
     for s in range(DESCENTS):
         last = s == DESCENTS - 1
-        take_z(s, fld, mu)
-        lsum = lax.fori_loop(3, cx + 1, omega_plane, zero)
+        lsum = inner_planes(s, fld, mu, omega_plane, zero)
         take_x(s, fld if s == 0 else fb2, fld, mu)
         lsum = over_edges(omega_plane, lsum, 1, 2)
 
@@ -382,10 +402,10 @@
             send_x(s + 1, fb2)
             pack_corners(s + 1, fb2)
             send_corners(s + 1)
-        gsum = lax.fori_loop(4, cx, force, gsum)
+            gsum = later_planes(s + 1, force, gsum)
+        else:
+            gsum = lax.fori_loop(4, cx, force, gsum)
         send_sums(s, lsum, gsum)
-        if not last:
-            send_z(s + 1)
         loop(2, cx + 2, lambda i: suffix_plane(i, fb2, eb))
         if last:
             loop(2, cx + 2, lambda i: column_plane(i, eb, 1), 2)
@@ -435,8 +455,7 @@
 
     over_edges(lift, 0, 2, 2)
     send_x(DESCENTS, pot)
-    lax.fori_loop(4, cx, lift, 0)
-    send_z(DESCENTS)
+    later_planes(DESCENTS, lift, 0)
     pack_corners(DESCENTS, pot)
     send_corners(DESCENTS)
     loop(2, cx + 2, update)
@@ -485,8 +504,7 @@
     for s in range(RELAX):
         r = DESCENTS + s
         last = s == RELAX - 1
-        take_z(r, pot, None)
-        lax.fori_loop(3, cx + 1, induced_plane, 0)
+        inner_planes(r, pot, None, induced_plane, 0)
         take_x(r, pot, pot, None)
         over_edges(induced_plane, 0, 1, 2)
 
@@ -503,8 +521,7 @@
             send_x(r + 1, pot)
             pack_corners(r + 1, pot)
             send_corners(r + 1)
-            lax.fori_loop(4, cx, relax, 0)
-            send_z(r + 1)
+            later_planes(r + 1, relax, 0)
 
     for b in range(nb):
         out_copy(pot, out_p, b, 1).start()
@@ -534,7 +551,7 @@
             VM(ROUNDS, 4, 3, nb, LANES), VM(ROUNDS, 4, 3, nb, LANES),
             VM(DESCENTS, 2, LANES), VM(DESCENTS, n, 2, LANES),
             VM(2, 2, cx, nb, LANES), VM(2, gzn, 2, cx, nb, LANES), VM(2, cx, nb, LANES),
-            DMA(ROUNDS, 2, 2), DMA(ROUNDS, 2, 2),
+            DMA(ROUNDS, 2, 2), DMA(ROUNDS, 2, 2), DMA(ROUNDS, 2, 2), DMA(ROUNDS, 2, 2),
             DMA(ROUNDS, 8), DMA(ROUNDS, 8),
             DMA(DESCENTS, n), DMA(DESCENTS, n), DMA(2, gzn), DMA(2, gzn), DMA(nb), DMA(2, nb),
         ],

time: 58.6 us -> 56.4 us (0.962)
  Pallas kernels: 53.5 us -> 51.2 us
    pallas_call x1, Pallas kernels: 53.5 us -> 51.2 us  [body(): pl.pallas_call(functools.partial(kernel, gxn, gzn, cx, cz, nb), out_shape...]
where the time goes in v4:
time: 56.4 us; the launch traced here: 56.2 us
  Pallas kernels  51.2 us (91%)
  local copies, waits for them, and re-layouts  4.34 us (8%)
  between operations  0.65 us (1%)
    pallas_call x1, Pallas kernels, body(): pl.pallas_call(functools.partial(kernel, gxn, gzn, cx, cz, nb), out_shape...  51.2 us
    unnamed x6, local copies, waits for them, and re-layouts  4.34 us

profile of v4, /device:TPU:1, one launch (start us, length us, event | category | flops | bytes accessed | tf_op | source)
XLA Modules:
  0.0 56.2 jit_solution(101848585065249651)
XLA Ops:
  0.6 0.0 copy-start
  0.6 1.4 %copy-done = f32[3,16,16,512]{3,2,1,0:T(8,128)S(1)} copy-done((f32[3,16,16,512]{3,2,1,0:T(8,128)S(1)}, f32[3,16,16,512]{3,2,1,0:T(8,128)}, u32[]{:S(2)}) %copy-start) | copy-done | bytes 1572888
  2.0 0.0 copy-start.1
  2.0 0.7 %copy-done.1 = f32[16]{0:T(128)S(1)} copy-done((f32[16]{0:T(128)S(1)}, f32[16]{0:T(128)}, u32[]{:S(2)}) %copy-start.1) | copy-done | bytes 88
  2.7 51.2 %shard_map.41 = (f32[3,16,16,512]{3,2,1,0:T(8,128)S(1)}, f32[3,16,16,512]{3,2,1,0:T(8,128)S(1)}) custom-call(f32[3,16,16,512]{3,2,1,0:T(8,128)S(1)} %copy-done, f32[16]{0:T(128)S(1)} %copy-done.1), custom_call_target="tpu_custom_call" | custom-call | tf_op jit(solution)/shard_map/pallas_call | solution.py:542
  53.9 1.1 %copy.6 = f32[3,16,16,512]{3,2,1,0:T(8,128)} copy(f32[3,16,16,512]{3,2,1,0:T(8,128)S(1)} %get-tuple-element.4) | data formatting | bytes 3145728
  55.1 1.1 %copy.7 = f32[3,16,16,512]{3,2,1,0:T(8,128)} copy(f32[3,16,16,512]{3,2,1,0:T(8,128)S(1)} %get-tuple-element.5) | data formatting | bytes 3145728
Async XLA Ops:
  0.6 1.4 %copy-start = (f32[3,16,16,512]{3,2,1,0:T(8,128)S(1)}, f32[3,16,16,512]{3,2,1,0:T(8,128)}, u32[]{:S(2)}) copy-start(f32[3,16,16,512]{3,2,1,0:T(8,128)} %mag.1) | copy-start | bytes 4718596
  2.0 0.7 %copy-start.1 = (f32[16]{0:T(128)S(1)}, f32[16]{0:T(128)}, u32[]{:S(2)}) copy-start(f32[16]{0:T(128)} %fric.1) | copy-start | bytes 196
